TPU v7x, 32 devices: a whole 2x2x4 slice. The times are simulated.
32 devices in a mesh: row: 2 (over y), col: 4 (over x, core), tm: 4 (over z).
Axes of the slice: x: 2, y: 2, z: 4, core: 2. Of those that a mesh axis runs over, the one named last changes fastest.
Arguments:
- filled_orbitals: bfloat16 [4, 1024, 1024], P('col', 'row', 'tm'), may hold values from -0.1875 to 0.1875
- empty_orbitals: bfloat16 [4, 1024, 3072], P('col', 'row', 'tm'), may hold values from -0.109375 to 0.109375
- filled_depth: bfloat16 [1024], P('tm'), may hold values from 0.019897461 to 2
- empty_depth: bfloat16 [3072], P('tm'), may hold values from 0.019897461 to 2
- time_points: float32 [4], P('tm'), may hold values from 0.05 to 8
- cosine_weights: float32 [4, 4], replicated, may hold values from -3 to 3
Outputs:
- polar_freq: float32 [4, 4, 1024, 4096], P(None, None, ('row', 'tm'), 'col')
All inputs are finite; a program needn't handle non-finite values.
Results may differ from a plain program's by a relative error of at most 0.0033.
Values may be sent and summed in bfloat16 or wider, within the bound.
No kernel may reach another device: no remote copies, remote signals or barrier semaphores. Data moves between devices by JAX's collectives and lax.ppermute only.
A program may use at most 128 MiB of HBM per device.

v0:
```python
import jax
import jax.numpy as jnp
from jax import lax
from jax.sharding import PartitionSpec as P


def tile_product(left_points, right_points, depths, tau_value):
    band_count = left_points.shape[-1]
    weight_row = jnp.exp(-depths.astype(jnp.float32) * tau_value)
    scaled = (
        right_points.reshape(-1, band_count).astype(jnp.float32) * weight_row[None, :]
    ).astype(jnp.bfloat16)
    return lax.dot_general(
        left_points.reshape(-1, band_count),
        scaled,
        (((1,), (1,)), ((), ())),
        preferred_element_type=jnp.float32,
    )


def on_device(
    filled_orbitals, empty_orbitals, filled_depth, empty_depth, time_points, cosine_weights
):
    tau_value = time_points[0]
    filled_bands, empty_bands, filled_all, empty_all = (
        lax.all_gather(filled_orbitals, "tm", axis=2, tiled=True),
        lax.all_gather(empty_orbitals, "tm", axis=2, tiled=True),
        lax.all_gather(filled_depth, "tm", axis=0, tiled=True),
        lax.all_gather(empty_depth, "tm", axis=0, tiled=True),
    )
    filled_rows, empty_rows = (
        lax.all_gather(filled_bands, "col", axis=0, tiled=True),
        lax.all_gather(empty_bands, "col", axis=0, tiled=True),
    )
    column_filled, column_empty = lax.all_gather(
        (filled_bands, empty_bands), "row", axis=1, tiled=True
    )
    green_filled = tile_product(filled_rows, column_filled, filled_all, tau_value)
    green_empty = tile_product(empty_rows, column_empty, empty_all, tau_value)
    polar_time = (
        (-(green_filled * green_empty))
        .astype(jnp.bfloat16)
        .reshape(filled_rows.shape[0], filled_rows.shape[1], -1)
    )
    return jnp.einsum(
        "ft,tabc->fabc",
        cosine_weights,
        lax.all_to_all(polar_time[None], "tm", split_axis=2, concat_axis=0, tiled=True).astype(
            jnp.float32
        ),
        precision=lax.Precision.HIGHEST,
    )


def solution(mesh):
    in_specs = (P("col", "row", "tm"), P("col", "row", "tm"), P("tm"), P("tm"), P("tm"), P())
    out_specs = P(None, None, ("row", "tm"), "col")
    return jax.shard_map(
        on_device, mesh=mesh, in_specs=in_specs, out_specs=out_specs, check_vma=False
    )
```

profile of v0, /device:TPU:0, one launch (start us, length us, event | category | flops | bytes accessed | tf_op | source)
XLA Modules:
  0.0 491.7 jit_solution(13205183618008928850)
XLA Ops:
  6.5 0.7 all-gather.15.cloned.1.call-update
  7.3 0.0 all-gather.9.cloned.1.call-start
  7.3 0.7 all-gather.9.cloned.1.call-update
  8.0 0.0 all-gather.17.cloned.1.call-start
  8.1 67.0 %all-gather.15.cloned.1.call-done = bf16[1,512,3072]{2,1,0:T(8,128)(2,1)} async-done(((bf16[1,512,768]{2,1,0:T(8,128)(2,1)}), bf16[1,512,3072]{2,1,0:T(8,128)(2,1)}) %all-gather.15.cloned.1.call-update) | async-done | bytes 3145744 | tf_op jit(solution)/shard_map/all_gather | solution.py:27
  75.1 0.0 all-gather.19.cloned.1.call-start
  75.2 0.5 all-gather.19.cloned.1.call-update
  75.7 0.0 all-gather.11.cloned.1.call-start
  75.8 29.5 %all-gather.9.cloned.1.call-done = bf16[1,512,1024]{2,1,0:T(8,128)(2,1)} async-done(((bf16[1,512,256]{2,1,0:T(8,128)(2,1)}), bf16[1,512,1024]{2,1,0:T(8,128)(2,1)}) %all-gather.9.cloned.1.call-update) | async-done | bytes 1048592 | tf_op jit(solution)/shard_map/all_gather | solution.py:26
  105.3 0.0 all-gather.13.cloned.1.call-start
  105.3 0.5 all-gather.13.cloned.1.call-update
  106.6 10.1 %all-gather = bf16[4,1,256]{2,1,0:T(2,128)(2,1)S(1)} all-gather(bf16[1,1,256]{2,1,0:T(2,128)(2,1)S(1)} %reshape.26), channel_id=1, replica_groups=mesh['row'=2,'col'=4,'tm'=4] {'tm'}, dimensions={0}, use_global_device_ids=true | all-gather | bytes 2560 | tf_op jit(solution)/shard_map/all_gather | solution.py:28
  116.7 13.1 %all-gather.1 = bf16[4,1,768]{2,1,0:T(2,128)(2,1)S(1)} all-gather(bf16[1,1,768]{2,1,0:T(2,128)(2,1)S(1)} %reshape.28), channel_id=1, replica_groups=mesh['row'=2,'col'=4,'tm'=4] {'tm'}, dimensions={0}, use_global_device_ids=true | all-gather | bytes 7680 | tf_op jit(solution)/shard_map/all_gather | solution.py:29
  129.8 55.7 %all-gather.17.cloned.1.call-done = bf16[1,1024,3072]{2,1,0:T(8,128)(2,1)} async-done(((bf16[1,512,3072]{2,1,0:T(8,128)(2,1)}), bf16[1,1024,3072]{2,1,0:T(8,128)(2,1)}) %all-gather.17.cloned.1.call-update) | async-done | bytes 6291472 | tf_op jit(solution)/shard_map/all_gather | solution.py:35
  185.5 83.5 %all-gather.19.cloned.1.call-done = bf16[4,512,3072]{2,1,0:T(8,128)(2,1)} async-done(((bf16[1,512,3072]{2,1,0:T(8,128)(2,1)}), bf16[4,512,3072]{2,1,0:T(8,128)(2,1)}) %all-gather.19.cloned.1.call-update) | async-done | bytes 12582928 | tf_op jit(solution)/shard_map/all_gather | solution.py:33
  269.0 18.9 %fusion.1 = f32[1024,2048]{1,0:T(8,128)} fusion(bf16[2048,3072]{1,0:T(8,128)(2,1)} %bitcast.35, bf16[1,1024,3072]{2,1,0:T(8,128)(2,1)} %all-gather.17.cloned.1.call-done, f32[3072]{0:T(1024)S(1)} %bitcast.33), kind=kOutput, calls=%fused_computation.3 | convolution fusion | flops 12894339072 | bytes 27275264 | tf_op jit(solution)/shard_map/dot_general | solution.py:13
  287.9 15.6 %all-gather.11.cloned.1.call-done = bf16[1,1024,1024]{2,1,0:T(8,128)(2,1)} async-done(((bf16[1,512,1024]{2,1,0:T(8,128)(2,1)}), bf16[1,1024,1024]{2,1,0:T(8,128)(2,1)}) %all-gather.11.cloned.1.call-update) | async-done | bytes 2097168 | tf_op jit(solution)/shard_map/all_gather | solution.py:35
  303.5 35.9 %all-gather.13.cloned.1.call-done = bf16[4,512,1024]{2,1,0:T(8,128)(2,1)} async-done(((bf16[1,512,1024]{2,1,0:T(8,128)(2,1)}), bf16[4,512,1024]{2,1,0:T(8,128)(2,1)}) %all-gather.13.cloned.1.call-update) | async-done | bytes 4194320 | tf_op jit(solution)/shard_map/all_gather | solution.py:32
  339.4 11.8 %fusion.6 = bf16[2048,1024]{0,1:T(8,128)(2,1)} fusion(f32[1024,2048]{1,0:T(8,128)} %fusion.1, bf16[2048,1024]{1,0:T(8,128)(2,1)} %bitcast.36, bf16[1,1024,1024]{2,1,0:T(8,128)(2,1)} %all-gather.11.cloned.1.call-done, f32[1024]{0:T(1024)S(1)} %bitcast.34), kind=kOutput, calls=%fused_computation.9 | convolution fusion | flops 4304404480 | bytes 18878464 | tf_op jit(solution)/shard_map/dot_general | solution.py:13
  351.2 7.8 %broadcast_in_dim_reshape.3 = bf16[1,4,512,1024]{2,1,3,0:T(4,128)(2,1)} reshape(bf16[2048,1024]{0,1:T(8,128)(2,1)} %fusion.6) | data formatting | bytes 8388608 | tf_op jit(solution)/shard_map/broadcast_in_dim;reshape | solution.py:48
  359.0 10.0 %copy.11 = bf16[1,4,512,1024]{3,1,0,2:T(4,128)(2,1)} copy(bf16[1,4,512,1024]{2,1,3,0:T(4,128)(2,1)} %broadcast_in_dim_reshape.3) | data formatting | bytes 8388608 | tf_op jit(solution)/shard_map/broadcast_in_dim;reshape | solution.py:48
  369.0 98.1 %all_to_all.18 = bf16[1,4,512,1024]{3,1,0,2:T(4,128)(2,1)S(1)} all-to-all(bf16[1,4,512,1024]{3,1,0,2:T(4,128)(2,1)} %copy.11), channel_id=1, replica_groups=mesh['row'=2,'col'=4,'tm'=4] {'tm'}, dimensions={2} | all-to-all | bytes 8388608 | tf_op jit(solution)/shard_map/all_to_all | solution.py:48
  467.2 9.4 %convolution_bitcast_fusion = f32[4,4,128,1024]{3,0,2,1:T(4,128)S(1)} fusion(bf16[1,4,4,128,1024]{4,1,3,2,0:T(4,128)(2,1)S(1)} %bitcast.32, f32[4,4]{1,0:T(4,128)S(1)} %copy-done), kind=kOutput, calls=%fused_computation.5 | convolution fusion | flops 100663296 | bytes 12582976 | tf_op jit(solution)/shard_map/ft,tabc->fabc/dot_general | solution.py:45
  476.6 8.3 %copy.14 = f32[4,4,128,1024]{3,2,1,0:T(8,128)} copy(f32[4,4,128,1024]{3,0,2,1:T(4,128)S(1)} %convolution_bitcast_fusion) | data formatting | bytes 16777216 | tf_op jit(solution)/shard_map/ft,tabc->fabc/dot_general | solution.py:45
  (13 shorter events, 0.1 us)
Async XLA Ops:
  6.5 460.6 %copy-start = (f32[4,4]{1,0:T(4,128)S(1)}, f32[4,4]{1,0:T(4,128)}, u32[]{:S(2)}) copy-start(f32[4,4]{1,0:T(4,128)} %param.11) | copy-start | bytes 196
  6.5 68.6 %all-gather.15.cloned.1.call-start = ((), (), s32[]{:S(2)}) async-start(), calls=%async_computation.4 | async-start | bytes 3932160 | tf_op jit(solution)/shard_map/all_gather | solution.py:27
  7.3 98.0 %all-gather.9.cloned.1.call-start = ((), (), s32[]{:S(2)}) async-start(), calls=%async_computation.1 | async-start | bytes 1310720 | tf_op jit(solution)/shard_map/all_gather | solution.py:26
  8.0 177.5 %all-gather.17.cloned.1.call-start = ((), (), s32[]{:S(2)}) async-start(), calls=%async_computation.5 | async-start | bytes 9437184 | tf_op jit(solution)/shard_map/all_gather | solution.py:35
  75.1 31.4 %copy-start.1 = (bf16[768]{0:T(1024)(128)(2,1)S(1)}, bf16[768]{0:T(1024)(128)(2,1)}, u32[]{:S(2)}) copy-start(bf16[768]{0:T(1024)(128)(2,1)} %param.9) | copy-start | bytes 4612
  75.1 31.4 %copy-start.2 = (bf16[256]{0:T(256)(128)(2,1)S(1)}, bf16[256]{0:T(256)(128)(2,1)}, u32[]{:S(2)}) copy-start(bf16[256]{0:T(256)(128)(2,1)} %param.8) | copy-start | bytes 1540
  75.1 193.9 %all-gather.19.cloned.1.call-start = ((), (), s32[]{:S(2)}) async-start(), calls=%async_computation.6 | async-start | bytes 15728640 | tf_op jit(solution)/shard_map/all_gather | solution.py:33
  75.7 227.8 %all-gather.11.cloned.1.call-start = ((), (), s32[]{:S(2)}) async-start(), calls=%async_computation.2 | async-start | bytes 3145728 | tf_op jit(solution)/shard_map/all_gather | solution.py:35
  105.3 234.2 %all-gather.13.cloned.1.call-start = ((), (), s32[]{:S(2)}) async-start(), calls=%async_computation.3 | async-start | bytes 5242880 | tf_op jit(solution)/shard_map/all_gather | solution.py:32
Sparse Core Ops, SparseCore 0:
  8.9 66.1 all-gather.14
  76.7 28.5 all-gather.8
  106.8 78.6 all-gather.16
  186.9 82.0 all-gather.18
  270.4 33.0 all-gather.10
  305.0 34.4 all-gather.12
where the time goes:
time: 492 us
  waiting for transfers between devices  290 us (59%)
  blocking collectives  121 us (25%)
  matrix products  40.1 us (8%)
  local copies, waits for them, and re-layouts  26.1 us (5%)
  between operations  14.2 us (3%)
    all_to_all x1, blocking collectives, on_device(): lax.all_to_all(polar_time[None], 'tm', split_axis=2, concat_axis=0, tiled...  98.1 us
    all_gather x1, waiting for transfers between devices, on_device(): lax.all_gather(empty_bands, 'col', axis=0, tiled=True)  83.5 us
    all_gather x2, waiting for transfers between devices, on_device(): lax.all_gather((filled_bands, empty_bands), 'row', axis=1, tiled=True)  71.3 us
    all_gather x1, waiting for transfers between devices, on_device(): lax.all_gather(empty_orbitals, 'tm', axis=2, tiled=True)  67 us
    all_gather x1, waiting for transfers between devices, on_device(): lax.all_gather(filled_bands, 'col', axis=0, tiled=True)  35.9 us
    dot_general x2, matrix products, tile_product(): lax.dot_general(left_points.reshape(-1, band_count), scaled, (((1,), (1,)...  30.6 us
    all_gather x1, waiting for transfers between devices, on_device(): lax.all_gather(filled_orbitals, 'tm', axis=2, tiled=True)  29.5 us
    another operation x2, local copies, waits for them, and re-layouts, on_device(): polar_time[None]  17.8 us
  transfers between devices with their start and end apart: 6, of which 6 were waited for; matrix products, arithmetic and copies ran while one was open for 4% of the time, Pallas kernels for 0%

commit v1 on v0

--- a/solution.py
+++ b/solution.py
@@ -2,6 +2,18 @@
 import jax.numpy as jnp
 from jax import lax
 from jax.sharding import PartitionSpec as P
+
+
+def collect(shard, axis, dim):
+    ways, here, step = (lax.axis_size(axis), lax.axis_index(axis), shard.shape[dim])
+    shape = [n * ways if d == dim else n for d, n in enumerate(shard.shape)]
+    full = lax.dynamic_update_slice_in_dim(
+        jnp.zeros(shape, shard.dtype), shard, here * step, axis=dim
+    )
+    for far in range(1, ways):
+        shard = lax.ppermute(shard, axis, [(d, (d + 1) % ways) for d in range(ways)])
+        full = lax.dynamic_update_slice_in_dim(full, shard, (here - far) % ways * step, axis=dim)
+    return full
 
 
 def tile_product(left_points, right_points, depths, tau_value):
@@ -29,7 +41,7 @@
         lax.all_gather(empty_depth, "tm", axis=0, tiled=True),
     )
     filled_rows, empty_rows = (
-        lax.all_gather(filled_bands, "col", axis=0, tiled=True),
+        collect(filled_bands, "col", 0),
         lax.all_gather(empty_bands, "col", axis=0, tiled=True),
     )
     column_filled, column_empty = lax.all_gather(

time: 492 us -> 438 us (0.89)
  waiting for transfers between devices: 290 us -> 245 us
  local copies, waits for them, and re-layouts: 26.1 us -> 19.5 us
    all_gather x2, waiting for transfers between devices: 71.3 us -> 34.7 us  [on_device(): lax.all_gather((filled_bands, empty_bands), 'row', axis=1, tiled=True)]
    all_gather x1 -> x0, waiting for transfers between devices: 35.9 us -> none  [on_device(): lax.all_gather(filled_bands, 'col', axis=0, tiled=True)]
    ppermute x0 -> x3, waiting for transfers between devices: none -> 28.7 us  [collect(): lax.ppermute(shard, axis, [(d, (d + 1) % ways) for d in range(ways)])]
    another operation x2 -> x1, local copies, waits for them, and re-layouts: 17.8 us -> 3.24 us  [on_device(): polar_time[None]]
    dynamic_update_slice x0 -> x4, local copies, waits for them, and re-layouts: none -> 5.43 us  [the longest x3 4.38 us: collect(): lax.dynamic_update_slice_in_dim(full, shard, (here - far) % ways * step,...]
  transfers between devices with their start and end apart: 6 -> 8, of which waited for: 6 -> 7; matrix products, arithmetic and copies ran while one was open for 4% -> 6% of each run, Pallas kernels for 0% -> 0%
where the time goes in v1:
time: 438 us
  waiting for transfers between devices  245 us (56%)
  blocking collectives  121 us (28%)
  matrix products  38.6 us (9%)
  local copies, waits for them, and re-layouts  19.5 us (4%)
  between operations  13.9 us (3%)
    all_to_all x1, blocking collectives, on_device(): lax.all_to_all(polar_time[None], 'tm', split_axis=2, concat_axis=0, tiled...  97.4 us
    all_gather x1, waiting for transfers between devices, on_device(): lax.all_gather(empty_bands, 'col', axis=0, tiled=True)  83.5 us
    all_gather x1, waiting for transfers between devices, on_device(): lax.all_gather(empty_orbitals, 'tm', axis=2, tiled=True)  67 us
    all_gather x2, waiting for transfers between devices, on_device(): lax.all_gather((filled_bands, empty_bands), 'row', axis=1, tiled=True)  34.7 us
    all_gather x1, waiting for transfers between devices, on_device(): lax.all_gather(filled_orbitals, 'tm', axis=2, tiled=True)  29.5 us
    dot_general x2, matrix products, tile_product(): lax.dot_general(left_points.reshape(-1, band_count), scaled, (((1,), (1,)...  29.2 us
    ppermute x3, waiting for transfers between devices, collect(): lax.ppermute(shard, axis, [(d, (d + 1) % ways) for d in range(ways)])  28.7 us
    all_gather x1, blocking collectives, on_device(): lax.all_gather(empty_depth, 'tm', axis=0, tiled=True)  13.1 us
  transfers between devices with their start and end apart: 8, of which 7 were waited for; matrix products, arithmetic and copies ran while one was open for 6% of the time, Pallas kernels for 0%

profile of v1, /device:TPU:0, one launch (start us, length us, event | category | flops | bytes accessed | tf_op | source)
XLA Modules:
  0.0 438.3 jit_solution(1217180541809440306)
XLA Ops:
  6.5 0.7 all-gather.12.cloned.1.call-update
  7.3 0.7 all-gather.8.cloned.1.call-update
  8.0 0.0 all-gather.14.cloned.1.call-start
  8.1 67.0 %all-gather.12.cloned.1.call-done = bf16[1,512,3072]{2,1,0:T(8,128)(2,1)} async-done(((bf16[1,512,768]{2,1,0:T(8,128)(2,1)}), bf16[1,512,3072]{2,1,0:T(8,128)(2,1)}) %all-gather.12.cloned.1.call-update) | async-done | bytes 3145744 | tf_op jit(solution)/shard_map/all_gather | solution.py:39
  75.2 0.5 all-gather.16.cloned.1.call-update
  75.8 29.5 %all-gather.8.cloned.1.call-done = bf16[1,512,1024]{2,1,0:T(8,128)(2,1)} async-done(((bf16[1,512,256]{2,1,0:T(8,128)(2,1)}), bf16[1,512,1024]{2,1,0:T(8,128)(2,1)}) %all-gather.8.cloned.1.call-update) | async-done | bytes 1048592 | tf_op jit(solution)/shard_map/all_gather | solution.py:38
  105.3 14.4 %collective-permute-done = bf16[1,512,1024]{2,1,0:T(8,128)(2,1)S(1)} collective-permute-done((bf16[1,512,1024]{2,1,0:T(8,128)(2,1)}, bf16[1,512,1024]{2,1,0:T(8,128)(2,1)S(1)}, u32[]{:S(2)}, u32[]{:S(2)}) %collective-permute-start) | collective-permute-done | bytes 1048608 | tf_op jit(solution)/shard_map/ppermute | solution.py:14
  119.7 14.2 %collective-permute-done.1 = bf16[1,512,1024]{2,1,0:T(8,128)(2,1)S(1)} collective-permute-done((bf16[1,512,1024]{2,1,0:T(8,128)(2,1)S(1)}, bf16[1,512,1024]{2,1,0:T(8,128)(2,1)S(1)}, u32[]{:S(2)}, u32[]{:S(2)}) %collective-permute-start.1) | collective-permute-done | bytes 1048608 | tf_op jit(solution)/shard_map/ppermute | solution.py:14
  134.6 10.1 %all-gather = bf16[4,1,256]{2,1,0:T(2,128)(2,1)S(1)} all-gather(bf16[1,1,256]{2,1,0:T(2,128)(2,1)S(1)} %reshape.26), channel_id=1, replica_groups=mesh['row'=2,'col'=4,'tm'=4] {'tm'}, dimensions={0}, use_global_device_ids=true | all-gather | bytes 2560 | tf_op jit(solution)/shard_map/all_gather | solution.py:40
  144.7 13.1 %all-gather.1 = bf16[4,1,768]{2,1,0:T(2,128)(2,1)S(1)} all-gather(bf16[1,1,768]{2,1,0:T(2,128)(2,1)S(1)} %reshape.28), channel_id=1, replica_groups=mesh['row'=2,'col'=4,'tm'=4] {'tm'}, dimensions={0}, use_global_device_ids=true | all-gather | bytes 7680 | tf_op jit(solution)/shard_map/all_gather | solution.py:41
  157.9 2.6 broadcast_in_dim.2
  160.5 1.0 constant_dynamic-update-slice_fusion.3
  161.6 1.1 constant_dynamic-update-slice_fusion.2
  162.6 1.0 constant_dynamic-update-slice_fusion.1
  163.7 2.3 constant_dynamic-update-slice_fusion
  166.0 19.6 %all-gather.14.cloned.1.call-done = bf16[1,1024,3072]{2,1,0:T(8,128)(2,1)} async-done(((bf16[1,512,3072]{2,1,0:T(8,128)(2,1)}), bf16[1,1024,3072]{2,1,0:T(8,128)(2,1)}) %all-gather.14.cloned.1.call-update) | async-done | bytes 6291472 | tf_op jit(solution)/shard_map/all_gather | solution.py:47
  185.5 83.5 %all-gather.16.cloned.1.call-done = bf16[4,512,3072]{2,1,0:T(8,128)(2,1)} async-done(((bf16[1,512,3072]{2,1,0:T(8,128)(2,1)}), bf16[4,512,3072]{2,1,0:T(8,128)(2,1)}) %all-gather.16.cloned.1.call-update) | async-done | bytes 12582928 | tf_op jit(solution)/shard_map/all_gather | solution.py:45
  269.0 19.4 %fusion.3 = f32[1024,2048]{0,1:T(8,128)} fusion(bf16[2048,3072]{1,0:T(8,128)(2,1)} %bitcast.39, bf16[1,1024,3072]{2,1,0:T(8,128)(2,1)} %all-gather.14.cloned.1.call-done, f32[3072]{0:T(1024)S(1)} %bitcast.37), kind=kOutput, calls=%fused_computation.5 | convolution fusion | flops 12894339072 | bytes 27275264 | tf_op jit(solution)/shard_map/dot_general | solution.py:25
  288.4 15.2 %all-gather.10.cloned.1.call-done = bf16[1,1024,1024]{2,1,0:T(8,128)(2,1)} async-done(((bf16[1,512,1024]{2,1,0:T(8,128)(2,1)}), bf16[1,1024,1024]{2,1,0:T(8,128)(2,1)}) %all-gather.10.cloned.1.call-update) | async-done | bytes 2097168 | tf_op jit(solution)/shard_map/all_gather | solution.py:47
  303.6 9.8 %fusion.1 = bf16[2048,1024]{1,0:T(8,128)(2,1)S(1)} fusion(f32[1024,2048]{0,1:T(8,128)} %fusion.3, bf16[2048,1024]{1,0:T(8,128)(2,1)} %bitcast, bf16[1,1024,1024]{2,1,0:T(8,128)(2,1)} %all-gather.10.cloned.1.call-done, f32[1024]{0:T(1024)S(1)} %bitcast.38), kind=kOutput, calls=%fused_computation.3 | convolution fusion | flops 4304404480 | bytes 18878464 | tf_op jit(solution)/shard_map/dot_general | solution.py:25
  313.4 3.2 copy.13
  316.6 97.4 %all_to_all.18 = bf16[1,4,512,1024]{3,1,0,2:T(4,128)(2,1)S(1)} all-to-all(bf16[1,4,512,1024]{3,1,0,2:T(4,128)(2,1)S(1)} %copy.13), channel_id=1, replica_groups=mesh['row'=2,'col'=4,'tm'=4] {'tm'}, dimensions={2} | all-to-all | bytes 8388608 | tf_op jit(solution)/shard_map/all_to_all | solution.py:60
  414.0 9.4 %convolution_bitcast_fusion = f32[4,4,128,1024]{3,0,2,1:T(4,128)S(1)} fusion(bf16[1,4,4,128,1024]{4,1,3,2,0:T(4,128)(2,1)S(1)} %bitcast.35, f32[4,4]{1,0:T(4,128)S(1)} %copy-done), kind=kOutput, calls=%fused_computation.7 | convolution fusion | flops 100663296 | bytes 12582976 | tf_op jit(solution)/shard_map/ft,tabc->fabc/dot_general | solution.py:57
  423.5 8.3 %copy.16 = f32[4,4,128,1024]{3,2,1,0:T(8,128)} copy(f32[4,4,128,1024]{3,0,2,1:T(4,128)S(1)} %convolution_bitcast_fusion) | data formatting | bytes 16777216 | tf_op jit(solution)/shard_map/ft,tabc->fabc/dot_general | solution.py:57
  (22 shorter events, 0.2 us)
Async XLA Ops:
  6.5 407.5 %copy-start = (f32[4,4]{1,0:T(4,128)S(1)}, f32[4,4]{1,0:T(4,128)}, u32[]{:S(2)}) copy-start(f32[4,4]{1,0:T(4,128)} %param.11) | copy-start | bytes 196
  6.5 127.4 %copy-start.2 = (bf16[768]{0:T(1024)(128)(2,1)S(1)}, bf16[768]{0:T(1024)(128)(2,1)}, u32[]{:S(2)}) copy-start(bf16[768]{0:T(1024)(128)(2,1)} %param.9) | copy-start | bytes 4612
  6.5 128.1 %copy-start.3 = (bf16[256]{0:T(256)(128)(2,1)S(1)}, bf16[256]{0:T(256)(128)(2,1)}, u32[]{:S(2)}) copy-start(bf16[256]{0:T(256)(128)(2,1)} %param.8) | copy-start | bytes 1540
  6.5 68.6 %all-gather.12.cloned.1.call-start = ((), (), s32[]{:S(2)}) async-start(), calls=%async_computation.3 | async-start | bytes 3932160 | tf_op jit(solution)/shard_map/all_gather | solution.py:39
  7.3 98.0 %all-gather.8.cloned.1.call-start = ((), (), s32[]{:S(2)}) async-start(), calls=%async_computation.1 | async-start | bytes 1310720 | tf_op jit(solution)/shard_map/all_gather | solution.py:38
  8.0 177.5 %all-gather.14.cloned.1.call-start = ((), (), s32[]{:S(2)}) async-start(), calls=%async_computation.4 | async-start | bytes 9437184 | tf_op jit(solution)/shard_map/all_gather | solution.py:47
  75.1 193.9 %all-gather.16.cloned.1.call-start = ((), (), s32[]{:S(2)}) async-start(), calls=%async_computation.5 | async-start | bytes 15728640 | tf_op jit(solution)/shard_map/all_gather | solution.py:45
  75.7 227.8 %all-gather.10.cloned.1.call-start = ((), (), s32[]{:S(2)}) async-start(), calls=%async_computation.2 | async-start | bytes 3145728 | tf_op jit(solution)/shard_map/all_gather | solution.py:47
  105.3 55.2 %copy-start.1 = (bf16[1,512,1024]{2,1,0:T(8,128)(2,1)S(1)}, bf16[1,512,1024]{2,1,0:T(8,128)(2,1)}, u32[]{:S(2)}) copy-start(bf16[1,512,1024]{2,1,0:T(8,128)(2,1)} %all-gather.8.cloned.1.call-done) | copy-start | bytes 3145732
  105.3 14.4 %collective-permute-start = (bf16[1,512,1024]{2,1,0:T(8,128)(2,1)}, bf16[1,512,1024]{2,1,0:T(8,128)(2,1)S(1)}, u32[]{:S(2)}, u32[]{:S(2)}) collective-permute-start(bf16[1,512,1024]{2,1,0:T(8,128)(2,1)} %all-gather.8.cloned.1.call-done), channel_id=1, source_target_pairs={{0,4},{4,8},{8,12},{12,0},{1,5},{5,9},{9,13},{13,1},{2,6},{6,10},{... | collective-permute-start | bytes 3145736 | tf_op jit(solution)/shard_map/ppermute | solution.py:14
  119.7 14.2 %collective-permute-start.1 = (bf16[1,512,1024]{2,1,0:T(8,128)(2,1)S(1)}, bf16[1,512,1024]{2,1,0:T(8,128)(2,1)S(1)}, u32[]{:S(2)}, u32[]{:S(2)}) collective-permute-start(bf16[1,512,1024]{2,1,0:T(8,128)(2,1)S(1)} %collective-permute-done), channel_id=1, source_target_pairs={{0,4},{4,8},{8,12},{12,0},{1,5},{5,9},{9,13},{13,1},{2,6},{6,10},{... | collective-permute-start | bytes 3145736 | tf_op jit(solution)/shard_map/ppermute | solution.py:14
  133.9 29.7 %collective-permute-start.2 = (bf16[1,512,1024]{2,1,0:T(8,128)(2,1)S(1)}, bf16[1,512,1024]{2,1,0:T(8,128)(2,1)}, u32[]{:S(2)}, u32[]{:S(2)}) collective-permute-start(bf16[1,512,1024]{2,1,0:T(8,128)(2,1)S(1)} %collective-permute-done.1), channel_id=1, source_target_pairs={{0,4},{4,8},{8,12},{12,0},{1,5},{5,9},{9,13},{13,1},{2,6},{6,10},{... | collective-permute-start | bytes 3145736 | tf_op jit(solution)/shard_map/ppermute | solution.py:14
Sparse Core Ops, SparseCore 0:
  8.9 66.1 all-gather.11
  76.7 28.5 all-gather.7
  106.8 78.6 all-gather.13
  186.9 82.0 all-gather.15
  270.4 33.0 all-gather.9
